TPU v7x, 512 devices: a whole 4x4x16 slice. The times are simulated.
512 devices in a mesh: dp: 8 (over x, y_lo), tm: 64 (over z, y_hi, core).
Axes of the slice: x: 4, y: 4 (y_hi: 2, y_lo: 2; y = y_hi * 2 + y_lo), z: 16, core: 2. Of those that a mesh axis runs over, the one named last changes fastest.
Arguments:
- features: bfloat16 [8, 8192, 1536], P('dp', 'tm'), may hold values from -8 to 8
- start_noise: bfloat16 [8, 8192, 1536], P('dp', 'tm'), may hold values from -1 to 1
- cotangent: bfloat16 [8, 8192, 1536], P('dp', 'tm'), may hold values from -0.0234375 to 0.0234375
- in_weight: bfloat16 [3072, 1536], P('tm'), may hold values from -0.15625 to 0.15625
- kernel: float32 [31, 1536], replicated, may hold values from -1 to 1
- bn_gain: float32 [1536], replicated, may hold values from 0.25 to 1.75
- bn_shift: float32 [1536], replicated, may hold values from -1 to 1
- ends: int32 [8], replicated, may hold values from 4096 to 8192
Outputs:
- perturbation: float32 [8, 8192, 1536], P('dp', 'tm')
- grad_kernel: float32 [31, 1536], P(None, 'tm')
- grad_norm: float32 [2, 1536], P(None, 'tm')
Inputs may be any that keep to these rules, and one draw needn't show every extreme that they name: `ends`: frames at or after an utterance's end are padding.
All inputs are finite; a program needn't handle non-finite values.
Results may differ from a plain program's by a relative error of at most 0.0059.
Values may be sent and summed in bfloat16 or wider, within the bound.
A program may use at most 128 MiB of HBM per device.

v0:
```python
import jax
import jax.numpy as jnp
from jax import lax
from jax.sharding import PartitionSpec as P

ASCENT = 2
noise_scale = 0.5
ascent_rate = 0.5
layer_epsilon = 1e-05
batch_epsilon = 1e-05
ascent_epsilon = 1e-06


def normalize(summed):
    centre = summed - jnp.mean(summed, axis=-1, keepdims=True)
    inverse = lax.rsqrt(jnp.mean(centre * centre, axis=-1, keepdims=True) + layer_epsilon)
    return (centre * inverse, inverse)


def lane_conv_forward(padded, kernel, out_length):
    result = jnp.zeros((padded.shape[0], out_length), jnp.float32)
    for offset in range(kernel.shape[0]):
        result = result + kernel[offset][:, None] * padded[:, offset : offset + out_length].astype(
            jnp.float32
        )
    return result


def lane_conv_input_grad(padded, kernel, out_length):
    tap_span = kernel.shape[0] - 1
    result = jnp.zeros((padded.shape[0], out_length), jnp.float32)
    for offset in range(kernel.shape[0]):
        start_col = tap_span - offset
        result = result + kernel[offset][:, None] * padded[
            :, start_col : start_col + out_length
        ].astype(jnp.float32)
    return result


def lane_kernel_grad(grad_bf, padded, out_length):
    grad_float = grad_bf.astype(jnp.float32)
    rows_list = []
    for offset in range(padded.shape[1] - out_length + 1):
        rows_list.append(
            jnp.sum(
                grad_float * padded[:, offset : offset + out_length].astype(jnp.float32), axis=1
            )
        )
    return jnp.stack(rows_list)


def reduce_kernel(partial_grad):
    return lax.psum(partial_grad, "dp")


def on_device(features, start_noise, cotangent, in_weight, kernel, bn_gain, bn_shift, ends):
    frame_rows = features.shape[1]
    model_width = features.shape[2]
    tap_count = kernel.shape[0]
    half_span = (tap_count - 1) // 2
    shard_count = lax.axis_size("tm")
    shard_index = lax.axis_index("tm")
    group_index = lax.axis_index("dp")
    slice_width = model_width // shard_count
    all_frames = frame_rows * shard_count
    utter_end = lax.dynamic_index_in_dim(ends, group_index, 0, keepdims=False)
    live_count = jnp.sum(ends).astype(jnp.float32)
    utter_length = utter_end.astype(jnp.float32)
    frame_ids = shard_index * frame_rows + jnp.arange(frame_rows, dtype=jnp.int32)
    live_frames = (frame_ids < utter_end).astype(jnp.float32)
    live_whole = (jnp.arange(all_frames, dtype=jnp.int32) < utter_end).astype(jnp.float32)
    channel_start = shard_index * slice_width
    kernel_slice = lax.dynamic_slice_in_dim(kernel, channel_start, slice_width, 1)
    gain_slice = lax.dynamic_slice_in_dim(bn_gain, channel_start, slice_width, 0)
    shift_slice = lax.dynamic_slice_in_dim(bn_shift, channel_start, slice_width, 0)
    weight_full = lax.all_gather(in_weight, "tm", axis=0, tiled=True)
    inputs = features[0].astype(jnp.float32)
    perturbation = noise_scale * start_noise[0].astype(jnp.float32) * live_frames[:, None]
    cot_channels = lax.all_to_all(
        jnp.transpose(cotangent[0])[None], "tm", split_axis=1, concat_axis=2, tiled=True
    )[0]
    upstream = live_whole[None, :] * cot_channels.astype(jnp.float32) / ASCENT
    kernel_total = jnp.zeros((tap_count, slice_width), jnp.float32)
    norm_total = jnp.zeros((2, slice_width), jnp.float32)
    for ascent_step in range(ASCENT):
        summed = inputs + perturbation
        normed, inverse = normalize(summed)
        hidden = lax.dot_general(
            normed.astype(jnp.bfloat16),
            weight_full,
            (((1,), (1,)), ((), ())),
            preferred_element_type=jnp.float32,
        )
        value_half = hidden[:, :model_width]
        gate_half = jax.nn.sigmoid(hidden[:, model_width:])
        glu = (value_half * gate_half * live_frames[:, None]).astype(jnp.bfloat16)
        glu_local = lax.all_to_all(
            jnp.transpose(glu)[None], "tm", split_axis=1, concat_axis=2, tiled=True
        )[0]
        padded = jnp.pad(glu_local, ((0, 0), (half_span, half_span)))
        conv_out = lane_conv_forward(padded, kernel_slice, all_frames)
        live_mask = live_whole[None, :]
        batch_mean = lax.psum(jnp.sum(live_mask * conv_out, axis=1), "dp") / live_count
        centred = conv_out - batch_mean[:, None]
        variance = lax.psum(jnp.sum(live_mask * centred * centred, axis=1), "dp") / live_count
        inv_std = lax.rsqrt(variance + batch_epsilon)[:, None]
        gain_now, shift_now = (gain_slice[:, None], shift_slice[:, None])
        scaled = centred * inv_std
        pre_act = gain_now * scaled + shift_now
        pre_sigmoid = jax.nn.sigmoid(pre_act)
        grad_pre = upstream * pre_sigmoid * (1.0 + pre_act * (1.0 - pre_sigmoid))
        shift_sum, gain_sum = lax.psum(
            (jnp.sum(grad_pre, axis=1), jnp.sum(grad_pre * scaled, axis=1)), "dp"
        )
        norm_total = norm_total + jnp.stack([gain_sum, shift_sum])
        grad_conv = (
            live_mask
            * inv_std
            * gain_now
            * (grad_pre - (shift_sum[:, None] + scaled * gain_sum[:, None]) / live_count)
        ).astype(jnp.bfloat16)
        kernel_part = lane_kernel_grad(grad_conv, padded, all_frames)
        kernel_total = kernel_total + reduce_kernel(kernel_part)
        if ascent_step + 1 < ASCENT:
            grad_pad = jnp.pad(grad_conv, ((0, 0), (half_span, half_span)))
            grad_local = (
                lane_conv_input_grad(grad_pad, kernel_slice, all_frames) * live_mask
            ).astype(jnp.bfloat16)
            grad_glu = jnp.transpose(
                lax.all_to_all(grad_local[None], "tm", split_axis=2, concat_axis=1, tiled=True)[0]
            )
            grad_float = grad_glu.astype(jnp.float32)
            grad_hidden = jnp.concatenate(
                [grad_float * gate_half, grad_float * value_half * gate_half * (1.0 - gate_half)],
                axis=1,
            ).astype(jnp.bfloat16)
            grad_normed = jnp.dot(grad_hidden, weight_full, preferred_element_type=jnp.float32)
            grad_sum = inverse * (
                grad_normed
                - jnp.mean(grad_normed, axis=-1, keepdims=True)
                - normed * jnp.mean(grad_normed * normed, axis=-1, keepdims=True)
            )
            direction = live_frames[:, None] * grad_sum
            square_total = lax.psum(jnp.sum(direction * direction), "tm")
            perturbation = perturbation + direction * (
                ascent_rate
                * jnp.sqrt(utter_length * model_width)
                / (jnp.sqrt(square_total) + ascent_epsilon)
            )
    return (perturbation[None], kernel_total, norm_total)


def solution(mesh):
    return jax.shard_map(
        on_device,
        mesh=mesh,
        in_specs=(
            P("dp", "tm", None),
            P("dp", "tm", None),
            P("dp", "tm", None),
            P("tm", None),
            P(),
            P(),
            P(),
            P(),
        ),
        out_specs=(P("dp", "tm", None), P(None, "tm"), P(None, "tm")),
        check_vma=False,
    )
```

profile of v0, /device:TPU:16, one launch (start us, length us, event | category | flops | bytes accessed | tf_op | source)
XLA Modules:
  0.0 742.7 jit_solution(14522599243444606599)
XLA Ops:
  9.2 6.1 copy.87
  15.8 8.8 %reduce.1 = bf16[1536,128]{1,0:T(8,128)(2,1)S(1)} reduce(bf16[1536,1,128]{2,1,0:T(2,128)(2,1)S(1)} %bitcast.268, bf16[]{:T(256)} %broadcast.129), dimensions={1}, to_apply=%bitcast.247.reduce_sub_computation | reduce | bytes 786434
  25.5 18.9 %all-to-all-start.1 = ((bf16[64,2,1536]{2,1,0:T(2,128)(2,1)}), bf16[64,2,1536]{2,1,0:T(2,128)(2,1)S(1)}, u32[]{:S(2)}, u32[]{:S(2)}) async-start(bf16[64,2,1536]{2,1,0:T(2,128)(2,1)} %reshape.112), calls=%async_computation.1 | async-start | bytes 786432 | tf_op jit(solution)/shard_map/all_to_all | solution.py:79
  47.0 140.4 %all-gather.2.cloned.1.call-done = bf16[3072,1536]{1,0:T(8,128)(2,1)} async-done(((bf16[48,1536]{1,0:T(8,128)(2,1)}), bf16[3072,1536]{1,0:T(8,128)(2,1)}) %all-gather.2.cloned.1.call-update) | async-done | bytes 9437200 | tf_op jit(solution)/shard_map/all_gather | solution.py:76
  187.4 6.9 fusion.162
  197.5 9.5 %reduce = bf16[1536,128]{1,0:T(8,128)(2,1)} reduce(bf16[1536,1,128]{2,1,0:T(2,128)(2,1)S(1)} %bitcast.270, bf16[]{:T(256)} %broadcast.129), dimensions={1}, to_apply=%bitcast.227.reduce_sub_computation | reduce | bytes 786434
  208.8 11.1 %all-to-all-start = ((bf16[64,2,1536]{2,1,0:T(2,128)(2,1)}), bf16[64,2,1536]{2,1,0:T(2,128)(2,1)}, u32[]{:S(2)}, u32[]{:S(2)}) async-start(bf16[64,2,1536]{2,1,0:T(2,128)(2,1)} %reshape.114), calls=%async_computation | async-start | bytes 786432 | tf_op jit(solution)/shard_map/all_to_all | solution.py:97
  230.5 17.4 %all-to-all-done = bf16[64,2,1536]{2,1,0:T(2,128)(2,1)} async-done(((bf16[64,2,1536]{2,1,0:T(2,128)(2,1)}), bf16[64,2,1536]{2,1,0:T(2,128)(2,1)}, u32[]{:S(2)}, u32[]{:S(2)}) %all-to-all-start) | async-done | bytes 393248 | tf_op jit(solution)/shard_map/all_to_all | solution.py:97
  251.5 6.0 multiply_reduce_fusion.6
  257.5 20.7 %psum.77 = f32[24]{0:T(128)} all-reduce(f32[24]{0:T(128)} %get-tuple-element.100), channel_id=1, replica_groups=mesh['dp'=8,'tm'=64] {'dp'}, use_global_device_ids=true, to_apply=%region_3.4 | all-reduce | flops 24 | bytes 192 | tf_op jit(solution)/shard_map/psum | solution.py:103
  281.0 16.6 %psum.78 = f32[24]{0:T(128)} all-reduce(f32[24]{0:T(128)} %fusion.60), channel_id=1, replica_groups=mesh['dp'=8,'tm'=64] {'dp'}, use_global_device_ids=true, to_apply=%region_6.7 | all-reduce | flops 24 | bytes 192 | tf_op jit(solution)/shard_map/psum | solution.py:105
  298.8 3.4 fusion.179
  302.2 18.9 %all-reduce.4 = (f32[24]{0:T(128)}, f32[24]{0:T(128)}) all-reduce(f32[24]{0:T(128)} %get-tuple-element.83, f32[24]{0:T(128)} %get-tuple-element.82), channel_id=1, replica_groups=mesh['dp'=8,'tm'=64] {'dp'}, use_global_device_ids=true, to_apply=%region_10.11 | all-reduce | flops 48 | bytes 384 | tf_op jit(solution)/shard_map/psum | solution.py:112
  325.1 5.4 fusion.174
  330.4 6.7 copy.52
  337.1 46.5 %reduce.2 = bf16[8192,24]{1,0:T(8,128)(2,1)} reduce(bf16[8192,1,24]{2,1,0:T(2,128)(2,1)} %bitcast.248, bf16[]{:T(256)} %broadcast.129), dimensions={1}, to_apply=%bitcast.229.reduce_sub_computation | reduce | bytes 786434
  383.6 4.9 reshape.116
  388.5 6.0 all-to-all-start.2
  395.2 27.1 %all-to-all-done.2 = bf16[64,2,1536]{2,1,0:T(2,128)(2,1)S(1)} async-done(((bf16[64,2,1536]{2,1,0:T(2,128)(2,1)}), bf16[64,2,1536]{2,1,0:T(2,128)(2,1)S(1)}, u32[]{:S(2)}, u32[]{:S(2)}) %all-to-all-start.2) | async-done | bytes 393248 | tf_op jit(solution)/shard_map/all_to_all | solution.py:130
  422.3 8.9 %reshape.117 = bf16[8192,1,24]{2,1,0:T(2,128)(2,1)} reshape(bf16[64,2,1536]{2,1,0:T(2,128)(2,1)S(1)} %all-to-all-done.2) | data formatting | bytes 786432
  431.2 8.0 %copy.53 = bf16[1,24,8192]{2,1,0:T(8,128)(2,1)S(1)} copy(bf16[1,24,8192]{1,0,2:T(2,128)(2,1)} %bitcast.249) | data formatting | bytes 786432 | tf_op jit(solution)/shard_map/all_to_all | solution.py:130
  442.5 5.3 fusion.178
  449.0 125.4 %psum.81 = f32[]{:T(128)} all-reduce(f32[]{:T(128)} %get-tuple-element.97), channel_id=1, replica_groups=mesh['dp'=8,'tm'=64] {'tm'}, use_global_device_ids=true, to_apply=%region_14.15 | all-reduce | flops 1 | bytes 8 | tf_op jit(solution)/shard_map/psum | solution.py:144
  576.5 6.8 fusion.165
  584.2 8.8 %reduce.3 = bf16[1536,128]{1,0:T(8,128)(2,1)S(1)} reduce(bf16[1536,1,128]{2,1,0:T(2,128)(2,1)S(1)} %bitcast.269, bf16[]{:T(256)} %broadcast.129), dimensions={1}, to_apply=%bitcast.231.reduce_sub_computation | reduce | bytes 786434
  593.8 11.3 %all-to-all-start.3 = ((bf16[64,2,1536]{2,1,0:T(2,128)(2,1)}), bf16[64,2,1536]{2,1,0:T(2,128)(2,1)S(1)}, u32[]{:S(2)}, u32[]{:S(2)}) async-start(bf16[64,2,1536]{2,1,0:T(2,128)(2,1)} %reshape.118), calls=%async_computation.3 | async-start | bytes 786432 | tf_op jit(solution)/shard_map/all_to_all | solution.py:97
  609.0 24.0 %all-to-all-done.3 = bf16[64,2,1536]{2,1,0:T(2,128)(2,1)S(1)} async-done(((bf16[64,2,1536]{2,1,0:T(2,128)(2,1)}), bf16[64,2,1536]{2,1,0:T(2,128)(2,1)S(1)}, u32[]{:S(2)}, u32[]{:S(2)}) %all-to-all-start.3) | async-done | bytes 393248 | tf_op jit(solution)/shard_map/all_to_all | solution.py:97
  633.7 6.0 multiply_reduce_fusion.1
  639.8 16.1 %psum.83 = f32[24]{0:T(128)S(1)} all-reduce(f32[24]{0:T(128)} %get-tuple-element.92), channel_id=1, replica_groups=mesh['dp'=8,'tm'=64] {'dp'}, use_global_device_ids=true, to_apply=%region_50.51 | all-reduce | flops 24 | bytes 192 | tf_op jit(solution)/shard_map/psum | solution.py:103
  656.9 18.0 %psum.84 = f32[24]{0:T(128)S(1)} all-reduce(f32[24]{0:T(128)S(1)} %fusion.61), channel_id=1, replica_groups=mesh['dp'=8,'tm'=64] {'dp'}, use_global_device_ids=true, to_apply=%region_52.53 | all-reduce | flops 24 | bytes 192 | tf_op jit(solution)/shard_map/psum | solution.py:105
  678.1 16.3 %all-reduce.3 = (f32[24]{0:T(128)S(1)}, f32[24]{0:T(128)S(1)}) all-reduce(f32[24]{0:T(128)} %get-tuple-element.49, f32[24]{0:T(128)} %get-tuple-element.48), channel_id=1, replica_groups=mesh['dp'=8,'tm'=64] {'dp'}, use_global_device_ids=true, to_apply=%region_56.57 | all-reduce | flops 48 | bytes 384 | tf_op jit(solution)/shard_map/psum | solution.py:112
  701.9 32.5 %psum.88 = f32[31,24]{1,0:T(8,128)S(1)} all-reduce(f32[31,24]{1,0:T(8,128)S(1)} %add.520), channel_id=1, replica_groups=mesh['dp'=8,'tm'=64] {'dp'}, use_global_device_ids=true, to_apply=%region_46.47 | all-reduce | flops 744 | bytes 5952 | tf_op jit(solution)/shard_map/psum | solution.py:53
  (162 shorter events, 56.9 us)
Async XLA Ops:
  7.2 37.2 %copy-start.46 = (s32[8]{0:T(128)S(1)}, s32[8]{0:T(128)}, u32[]{:S(2)}) copy-start(s32[8]{0:T(128)} %param.15) | copy-start | bytes 100
  7.2 38.5 %copy-start.1 = (bf16[1,128,1536]{2,1,0:T(8,128)(2,1)S(1)}, bf16[1,128,1536]{2,1,0:T(8,128)(2,1)}, u32[]{:S(2)}) copy-start(bf16[1,128,1536]{2,1,0:T(8,128)(2,1)} %param.8) | copy-start | bytes 1179652
  7.2 38.5 %copy-start = (bf16[1,128,1536]{2,1,0:T(8,128)(2,1)S(1)}, bf16[1,128,1536]{2,1,0:T(8,128)(2,1)}, u32[]{:S(2)}) copy-start(bf16[1,128,1536]{2,1,0:T(8,128)(2,1)} %param.9) | copy-start | bytes 1179652
  7.2 180.2 %all-gather.2.cloned.1.call-start = ((), (), s32[]{:S(2)}) async-start(), calls=%async_computation.4 | async-start | bytes 9584640 | tf_op jit(solution)/shard_map/all_gather | solution.py:76
  25.5 183.3 %all-to-all-start.1 = ((bf16[64,2,1536]{2,1,0:T(2,128)(2,1)}), bf16[64,2,1536]{2,1,0:T(2,128)(2,1)S(1)}, u32[]{:S(2)}, u32[]{:S(2)}) async-start(bf16[64,2,1536]{2,1,0:T(2,128)(2,1)} %reshape.112), calls=%async_computation.1 | async-start | bytes 786432 | tf_op jit(solution)/shard_map/all_to_all | solution.py:79
  46.0 148.3 %copy-start.11 = (f32[128]{0:T(128)}, f32[128]{0:T(128)S(1)}, u32[]{:S(2)}) copy-start(f32[128]{0:T(128)S(1)} %broadcast_multiply_fusion.3) | copy-start | bytes 1540
  46.6 147.7 %copy-start.8 = (f32[128]{0:T(128)}, f32[128]{0:T(128)S(1)}, u32[]{:S(2)}) copy-start(f32[128]{0:T(128)S(1)} %compare_convert_fusion) | copy-start | bytes 1540
  47.0 147.3 %copy-start.40 = (f32[128]{0:T(128)}, f32[128]{0:T(128)S(1)}, u32[]{:S(2)}) copy-start(f32[128]{0:T(128)S(1)} %add_rsqrt_fusion.3) | copy-start | bytes 1540
  208.8 39.0 %all-to-all-start = ((bf16[64,2,1536]{2,1,0:T(2,128)(2,1)}), bf16[64,2,1536]{2,1,0:T(2,128)(2,1)}, u32[]{:S(2)}, u32[]{:S(2)}) async-start(bf16[64,2,1536]{2,1,0:T(2,128)(2,1)} %reshape.114), calls=%async_computation | async-start | bytes 786432 | tf_op jit(solution)/shard_map/all_to_all | solution.py:97
  388.5 33.8 %all-to-all-start.2 = ((bf16[64,2,1536]{2,1,0:T(2,128)(2,1)}), bf16[64,2,1536]{2,1,0:T(2,128)(2,1)S(1)}, u32[]{:S(2)}, u32[]{:S(2)}) async-start(bf16[64,2,1536]{2,1,0:T(2,128)(2,1)} %reshape.116), calls=%async_computation.2 | async-start | bytes 786432 | tf_op jit(solution)/shard_map/all_to_all | solution.py:130
  584.2 49.6 %copy-start.7 = (f32[24]{0:T(128)S(1)}, f32[24]{0:T(128)}, u32[]{:S(2)}) copy-start(f32[24]{0:T(128)} %get-tuple-element.108) | copy-start | bytes 292
  593.8 81.0 %copy-start.4 = (f32[1,24,64,128]{3,2,1,0:T(8,128)S(1)}, f32[1,24,64,128]{3,2,1,0:T(8,128)}, u32[]{:S(2)}) copy-start(f32[1,24,64,128]{3,2,1,0:T(8,128)} %copy.51) | copy-start | bytes 2359300
  593.8 39.2 %all-to-all-start.3 = ((bf16[64,2,1536]{2,1,0:T(2,128)(2,1)}), bf16[64,2,1536]{2,1,0:T(2,128)(2,1)S(1)}, u32[]{:S(2)}, u32[]{:S(2)}) async-start(bf16[64,2,1536]{2,1,0:T(2,128)(2,1)} %reshape.118), calls=%async_computation.3 | async-start | bytes 786432 | tf_op jit(solution)/shard_map/all_to_all | solution.py:97
  633.7 66.2 %copy-start.6 = (bf16[1,24,64,128]{3,2,1,0:T(8,128)(2,1)S(1)}, bf16[1,24,64,128]{3,2,1,0:T(8,128)(2,1)}, u32[]{:S(2)}) copy-start(bf16[1,24,64,128]{3,2,1,0:T(8,128)(2,1)} %copy-done.5) | copy-start | bytes 1179652
  674.9 26.6 %copy-start.13 = (f32[24]{0:T(128)S(1)}, f32[24]{0:T(128)}, u32[]{:S(2)}) copy-start(f32[24]{0:T(128)} %get-tuple-element.50) | copy-start | bytes 292
  674.9 26.6 %copy-start.14 = (f32[24]{0:T(128)S(1)}, f32[24]{0:T(128)}, u32[]{:S(2)}) copy-start(f32[24]{0:T(128)} %get-tuple-element.51) | copy-start | bytes 292
  674.9 26.6 %copy-start.15 = (f32[24]{0:T(128)S(1)}, f32[24]{0:T(128)}, u32[]{:S(2)}) copy-start(f32[24]{0:T(128)} %get-tuple-element.52) | copy-start | bytes 292
  677.9 23.7 %copy-start.19 = (f32[24]{0:T(128)S(1)}, f32[24]{0:T(128)}, u32[]{:S(2)}) copy-start(f32[24]{0:T(128)} %get-tuple-element.56) | copy-start | bytes 292
  677.9 23.7 %copy-start.20 = (f32[24]{0:T(128)S(1)}, f32[24]{0:T(128)}, u32[]{:S(2)}) copy-start(f32[24]{0:T(128)} %get-tuple-element.57) | copy-start | bytes 292
  677.9 23.7 %copy-start.21 = (f32[24]{0:T(128)S(1)}, f32[24]{0:T(128)}, u32[]{:S(2)}) copy-start(f32[24]{0:T(128)} %get-tuple-element.58) | copy-start | bytes 292
  677.9 23.7 %copy-start.22 = (f32[24]{0:T(128)S(1)}, f32[24]{0:T(128)}, u32[]{:S(2)}) copy-start(f32[24]{0:T(128)} %get-tuple-element.59) | copy-start | bytes 292
  677.9 23.7 %copy-start.23 = (f32[24]{0:T(128)S(1)}, f32[24]{0:T(128)}, u32[]{:S(2)}) copy-start(f32[24]{0:T(128)} %get-tuple-element.60) | copy-start | bytes 292
  677.9 23.7 %copy-start.24 = (f32[24]{0:T(128)S(1)}, f32[24]{0:T(128)}, u32[]{:S(2)}) copy-start(f32[24]{0:T(128)} %get-tuple-element.61) | copy-start | bytes 292
  677.9 23.7 %copy-start.25 = (f32[24]{0:T(128)S(1)}, f32[24]{0:T(128)}, u32[]{:S(2)}) copy-start(f32[24]{0:T(128)} %get-tuple-element.62) | copy-start | bytes 292
  677.9 23.7 %copy-start.26 = (f32[24]{0:T(128)S(1)}, f32[24]{0:T(128)}, u32[]{:S(2)}) copy-start(f32[24]{0:T(128)} %get-tuple-element.63) | copy-start | bytes 292
  677.9 23.7 %copy-start.27 = (f32[24]{0:T(128)S(1)}, f32[24]{0:T(128)}, u32[]{:S(2)}) copy-start(f32[24]{0:T(128)} %get-tuple-element.64) | copy-start | bytes 292
  678.0 23.7 %copy-start.28 = (f32[24]{0:T(128)S(1)}, f32[24]{0:T(128)}, u32[]{:S(2)}) copy-start(f32[24]{0:T(128)} %get-tuple-element.65) | copy-start | bytes 292
  678.0 23.7 %copy-start.29 = (f32[24]{0:T(128)S(1)}, f32[24]{0:T(128)}, u32[]{:S(2)}) copy-start(f32[24]{0:T(128)} %get-tuple-element.66) | copy-start | bytes 292
  678.0 23.7 %copy-start.30 = (f32[24]{0:T(128)S(1)}, f32[24]{0:T(128)}, u32[]{:S(2)}) copy-start(f32[24]{0:T(128)} %get-tuple-element.67) | copy-start | bytes 292
  678.0 23.7 %copy-start.31 = (f32[24]{0:T(128)S(1)}, f32[24]{0:T(128)}, u32[]{:S(2)}) copy-start(f32[24]{0:T(128)} %get-tuple-element.68) | copy-start | bytes 292
  678.1 56.9 %copy-start.44 = (f32[24]{0:T(128)S(1)}, f32[24]{0:T(128)}, u32[]{:S(2)}) copy-start(f32[24]{0:T(128)} %get-tuple-element.88) | copy-start | bytes 292
  678.1 56.9 %copy-start.45 = (f32[24]{0:T(128)S(1)}, f32[24]{0:T(128)}, u32[]{:S(2)}) copy-start(f32[24]{0:T(128)} %get-tuple-element.89) | copy-start | bytes 292
  (20 other events, 304.0 us)
Sparse Core Ops, SparseCore 0:
  11.3 176.0 all-gather.1
where the time goes:
time: 750 us; the launch traced here: 743 us
  blocking collectives  264 us (35%)
  waiting for transfers between devices  210 us (28%)
  other arithmetic  125 us (17%)
  local copies, waits for them, and re-layouts  60.1 us (8%)
  starting transfers between devices  47.4 us (6%)
  matrix products  19 us (3%)
  between operations  17.2 us (2%)
    all_gather x1, waiting for transfers between devices, on_device(): weight_full = lax.all_gather(in_weight, 'tm', axis=0, tiled=True)  140 us
    psum x1, blocking collectives, on_device(): square_total = lax.psum(jnp.sum(direction * direction), 'tm')  125 us
    unnamed x5, other arithmetic  73.6 us
    all_to_all x2, waiting for transfers between devices, on_device(): lax.all_to_all(jnp.transpose(glu)[None], 'tm', split_axis=1, concat_axis=...  41.4 us
    psum x2, blocking collectives, on_device(): lax.psum(jnp.sum(live_mask * conv_out, axis=1), 'dp') / live_count  36.8 us
    psum x2, blocking collectives, on_device(): lax.psum((jnp.sum(grad_pre, axis=1), jnp.sum(grad_pre * scaled, axis=1)),...  35.2 us
    psum x2, blocking collectives, on_device(): lax.psum(jnp.sum(live_mask * centred * centred, axis=1), 'dp') / live_count  34.5 us
    psum x1, blocking collectives, reduce_kernel(): return lax.psum(partial_grad, 'dp')  32.5 us
  transfers between devices with their start and end apart: 5, of which 4 were waited for; matrix products, arithmetic and copies ran while one was open for 7% of the time, Pallas kernels for 0%

commit v1 on v0

--- a/solution.py
+++ b/solution.py
@@ -100,7 +100,10 @@
         padded = jnp.pad(glu_local, ((0, 0), (half_span, half_span)))
         conv_out = lane_conv_forward(padded, kernel_slice, all_frames)
         live_mask = live_whole[None, :]
-        batch_mean = lax.psum(jnp.sum(live_mask * conv_out, axis=1), "dp") / live_count
+        batch_mean = (
+            jnp.sum(lax.all_gather(jnp.sum(live_mask * conv_out, axis=1), "dp"), axis=0)
+            / live_count
+        )
         centred = conv_out - batch_mean[:, None]
         variance = lax.psum(jnp.sum(live_mask * centred * centred, axis=1), "dp") / live_count
         inv_std = lax.rsqrt(variance + batch_epsilon)[:, None]

time: 750 us -> 753 us (level)
    psum x2 -> x0, blocking collectives: 36.8 us -> none  [on_device(): lax.psum(jnp.sum(live_mask * conv_out, axis=1), 'dp') / live_count]
    unnamed x0 -> x2, blocking collectives: none -> 36.6 us
    unnamed x110 -> x119, local copies, waits for them, and re-layouts: 26.4 us -> 29.3 us
  transfers between devices with their start and end apart: 5 -> 5, of which waited for: 4 -> 4; matrix products, arithmetic and copies ran while one was open for 7% -> 8% of each run, Pallas kernels for 0% -> 0%
where the time goes in v1:
time: 753 us; the launch traced here: 745 us
  blocking collectives  264 us (35%)
  waiting for transfers between devices  208 us (28%)
  other arithmetic  126 us (17%)
  local copies, waits for them, and re-layouts  63.8 us (8%)
  starting transfers between devices  47.2 us (6%)
  matrix products  19 us (3%)
  between operations  17.9 us (2%)
    all_gather x1, waiting for transfers between devices, on_device(): weight_full = lax.all_gather(in_weight, 'tm', axis=0, tiled=True)  140 us
    psum x1, blocking collectives, on_device(): square_total = lax.psum(jnp.sum(direction * direction), 'tm')  125 us
    unnamed x5, other arithmetic  73.6 us
    all_to_all x2, waiting for transfers between devices, on_device(): lax.all_to_all(jnp.transpose(glu)[None], 'tm', split_axis=1, concat_axis=...  39.4 us
    unnamed x2, blocking collectives  36.6 us
    psum x2, blocking collectives, on_device(): lax.psum((jnp.sum(grad_pre, axis=1), jnp.sum(grad_pre * scaled, axis=1)),...  35 us
    psum x2, blocking collectives, on_device(): lax.psum(jnp.sum(live_mask * centred * centred, axis=1), 'dp') / live_count  34.7 us
    psum x1, blocking collectives, reduce_kernel(): return lax.psum(partial_grad, 'dp')  32.5 us
  transfers between devices with their start and end apart: 5, of which 4 were waited for; matrix products, arithmetic and copies ran while one was open for 8% of the time, Pallas kernels for 0%

profile of v1, /device:TPU:16, one launch (start us, length us, event | category | flops | bytes accessed | tf_op | source)
XLA Modules:
  0.0 745.5 jit_solution(96120503750794459)
XLA Ops:
  9.2 6.1 copy.100
  15.8 8.8 %reduce.1 = bf16[1536,128]{1,0:T(8,128)(2,1)S(1)} reduce(bf16[1536,1,128]{2,1,0:T(2,128)(2,1)S(1)} %bitcast.269, bf16[]{:T(256)} %broadcast.137), dimensions={1}, to_apply=%bitcast.248.reduce_sub_computation | reduce | bytes 786434
  25.5 18.9 %all-to-all-start.1 = ((bf16[64,2,1536]{2,1,0:T(2,128)(2,1)}), bf16[64,2,1536]{2,1,0:T(2,128)(2,1)S(1)}, u32[]{:S(2)}, u32[]{:S(2)}) async-start(bf16[64,2,1536]{2,1,0:T(2,128)(2,1)} %reshape.128), calls=%async_computation.1 | async-start | bytes 786432 | tf_op jit(solution)/shard_map/all_to_all | solution.py:79
  46.9 140.4 %all-gather.4.cloned.1.call-done = bf16[3072,1536]{1,0:T(8,128)(2,1)} async-done(((bf16[48,1536]{1,0:T(8,128)(2,1)}), bf16[3072,1536]{1,0:T(8,128)(2,1)}) %all-gather.4.cloned.1.call-update) | async-done | bytes 9437200 | tf_op jit(solution)/shard_map/all_gather | solution.py:76
  187.4 6.9 fusion.162
  197.5 9.5 %reduce = bf16[1536,128]{1,0:T(8,128)(2,1)} reduce(bf16[1536,1,128]{2,1,0:T(2,128)(2,1)S(1)} %bitcast.271, bf16[]{:T(256)} %broadcast.137), dimensions={1}, to_apply=%bitcast.228.reduce_sub_computation | reduce | bytes 786434
  208.8 11.1 %all-to-all-start = ((bf16[64,2,1536]{2,1,0:T(2,128)(2,1)}), bf16[64,2,1536]{2,1,0:T(2,128)(2,1)}, u32[]{:S(2)}, u32[]{:S(2)}) async-start(bf16[64,2,1536]{2,1,0:T(2,128)(2,1)} %reshape.130), calls=%async_computation | async-start | bytes 786432 | tf_op jit(solution)/shard_map/all_to_all | solution.py:97
  232.4 15.4 %all-to-all-done = bf16[64,2,1536]{2,1,0:T(2,128)(2,1)} async-done(((bf16[64,2,1536]{2,1,0:T(2,128)(2,1)}), bf16[64,2,1536]{2,1,0:T(2,128)(2,1)}, u32[]{:S(2)}, u32[]{:S(2)}) %all-to-all-start) | async-done | bytes 393248 | tf_op jit(solution)/shard_map/all_to_all | solution.py:97
  251.6 6.0 multiply_reduce_fusion.6
  258.3 20.7 %all-reduce.3 = f32[192]{0:T(256)} all-reduce(f32[192]{0:T(256)S(1)} %dynamic-update-slice), channel_id=2, replica_groups=mesh['dp'=8,'tm'=64] {'dp'}, use_global_device_ids=true, to_apply=%add.3 | all-reduce | flops 192 | bytes 1536
  283.1 16.8 %psum.63 = f32[24]{0:T(128)} all-reduce(f32[24]{0:T(128)} %fusion.60), channel_id=1, replica_groups=mesh['dp'=8,'tm'=64] {'dp'}, use_global_device_ids=true, to_apply=%region_6.7 | all-reduce | flops 24 | bytes 192 | tf_op jit(solution)/shard_map/psum | solution.py:108
  301.0 3.3 fusion.179
  304.4 18.6 %all-reduce.6 = (f32[24]{0:T(128)}, f32[24]{0:T(128)}) all-reduce(f32[24]{0:T(128)} %get-tuple-element.86, f32[24]{0:T(128)} %get-tuple-element.85), channel_id=1, replica_groups=mesh['dp'=8,'tm'=64] {'dp'}, use_global_device_ids=true, to_apply=%region_10.11 | all-reduce | flops 48 | bytes 384 | tf_op jit(solution)/shard_map/psum | solution.py:115
  327.1 5.4 fusion.174
  332.4 6.7 copy.65
  339.1 46.5 %reduce.2 = bf16[8192,24]{1,0:T(8,128)(2,1)} reduce(bf16[8192,1,24]{2,1,0:T(2,128)(2,1)} %bitcast.249, bf16[]{:T(256)} %broadcast.137), dimensions={1}, to_apply=%bitcast.230.reduce_sub_computation | reduce | bytes 786434
  385.6 4.9 reshape.132
  390.5 5.8 all-to-all-start.2
  397.0 27.3 %all-to-all-done.2 = bf16[64,2,1536]{2,1,0:T(2,128)(2,1)S(1)} async-done(((bf16[64,2,1536]{2,1,0:T(2,128)(2,1)}), bf16[64,2,1536]{2,1,0:T(2,128)(2,1)S(1)}, u32[]{:S(2)}, u32[]{:S(2)}) %all-to-all-start.2) | async-done | bytes 393248 | tf_op jit(solution)/shard_map/all_to_all | solution.py:133
  424.3 8.9 %reshape.133 = bf16[8192,1,24]{2,1,0:T(2,128)(2,1)} reshape(bf16[64,2,1536]{2,1,0:T(2,128)(2,1)S(1)} %all-to-all-done.2) | data formatting | bytes 786432
  433.2 8.0 %copy.66 = bf16[1,24,8192]{2,1,0:T(8,128)(2,1)S(1)} copy(bf16[1,24,8192]{1,0,2:T(2,128)(2,1)} %bitcast.250) | data formatting | bytes 786432 | tf_op jit(solution)/shard_map/all_to_all | solution.py:133
  444.5 5.3 fusion.178
  451.0 125.4 %psum.66 = f32[]{:T(128)} all-reduce(f32[]{:T(128)} %get-tuple-element.100), channel_id=1, replica_groups=mesh['dp'=8,'tm'=64] {'tm'}, use_global_device_ids=true, to_apply=%region_14.15 | all-reduce | flops 1 | bytes 8 | tf_op jit(solution)/shard_map/psum | solution.py:147
  578.5 6.8 fusion.165
  586.1 8.8 %reduce.3 = bf16[1536,128]{1,0:T(8,128)(2,1)S(1)} reduce(bf16[1536,1,128]{2,1,0:T(2,128)(2,1)S(1)} %bitcast.270, bf16[]{:T(256)} %broadcast.137), dimensions={1}, to_apply=%bitcast.232.reduce_sub_computation | reduce | bytes 786434
  595.8 11.3 %all-to-all-start.3 = ((bf16[64,2,1536]{2,1,0:T(2,128)(2,1)}), bf16[64,2,1536]{2,1,0:T(2,128)(2,1)S(1)}, u32[]{:S(2)}, u32[]{:S(2)}) async-start(bf16[64,2,1536]{2,1,0:T(2,128)(2,1)} %reshape.134), calls=%async_computation.3 | async-start | bytes 786432 | tf_op jit(solution)/shard_map/all_to_all | solution.py:97
  611.0 24.0 %all-to-all-done.3 = bf16[64,2,1536]{2,1,0:T(2,128)(2,1)S(1)} async-done(((bf16[64,2,1536]{2,1,0:T(2,128)(2,1)}), bf16[64,2,1536]{2,1,0:T(2,128)(2,1)S(1)}, u32[]{:S(2)}, u32[]{:S(2)}) %all-to-all-start.3) | async-done | bytes 393248 | tf_op jit(solution)/shard_map/all_to_all | solution.py:97
  635.7 6.0 multiply_reduce_fusion.1
  642.6 15.9 %all-reduce.4 = f32[192]{0:T(256)S(1)} all-reduce(f32[192]{0:T(256)S(1)} %dynamic-update-slice.1), channel_id=3, replica_groups=mesh['dp'=8,'tm'=64] {'dp'}, use_global_device_ids=true, to_apply=%add.4 | all-reduce | flops 192 | bytes 1536
  659.7 18.0 %psum.68 = f32[24]{0:T(128)S(1)} all-reduce(f32[24]{0:T(128)S(1)} %fusion.61), channel_id=1, replica_groups=mesh['dp'=8,'tm'=64] {'dp'}, use_global_device_ids=true, to_apply=%region_52.53 | all-reduce | flops 24 | bytes 192 | tf_op jit(solution)/shard_map/psum | solution.py:108
  680.9 16.3 %all-reduce.5 = (f32[24]{0:T(128)S(1)}, f32[24]{0:T(128)S(1)}) all-reduce(f32[24]{0:T(128)} %get-tuple-element.52, f32[24]{0:T(128)} %get-tuple-element.51), channel_id=1, replica_groups=mesh['dp'=8,'tm'=64] {'dp'}, use_global_device_ids=true, to_apply=%region_56.57 | all-reduce | flops 48 | bytes 384 | tf_op jit(solution)/shard_map/psum | solution.py:115
  704.7 32.5 %psum.72 = f32[31,24]{1,0:T(8,128)S(1)} all-reduce(f32[31,24]{1,0:T(8,128)S(1)} %add.516), channel_id=1, replica_groups=mesh['dp'=8,'tm'=64] {'dp'}, use_global_device_ids=true, to_apply=%region_46.47 | all-reduce | flops 744 | bytes 5952 | tf_op jit(solution)/shard_map/psum | solution.py:53
  (175 shorter events, 61.3 us)
Async XLA Ops:
  7.2 37.2 %copy-start.48 = (s32[8]{0:T(128)S(1)}, s32[8]{0:T(128)}, u32[]{:S(2)}) copy-start(s32[8]{0:T(128)} %param.15) | copy-start | bytes 100
  7.2 38.4 %copy-start.1 = (bf16[1,128,1536]{2,1,0:T(8,128)(2,1)S(1)}, bf16[1,128,1536]{2,1,0:T(8,128)(2,1)}, u32[]{:S(2)}) copy-start(bf16[1,128,1536]{2,1,0:T(8,128)(2,1)} %param.8) | copy-start | bytes 1179652
  7.2 38.4 %copy-start = (bf16[1,128,1536]{2,1,0:T(8,128)(2,1)S(1)}, bf16[1,128,1536]{2,1,0:T(8,128)(2,1)}, u32[]{:S(2)}) copy-start(bf16[1,128,1536]{2,1,0:T(8,128)(2,1)} %param.9) | copy-start | bytes 1179652
  7.2 180.2 %all-gather.4.cloned.1.call-start = ((), (), s32[]{:S(2)}) async-start(), calls=%async_computation.4 | async-start | bytes 9584640 | tf_op jit(solution)/shard_map/all_gather | solution.py:76
  25.5 183.4 %all-to-all-start.1 = ((bf16[64,2,1536]{2,1,0:T(2,128)(2,1)}), bf16[64,2,1536]{2,1,0:T(2,128)(2,1)S(1)}, u32[]{:S(2)}, u32[]{:S(2)}) async-start(bf16[64,2,1536]{2,1,0:T(2,128)(2,1)} %reshape.128), calls=%async_computation.1 | async-start | bytes 786432 | tf_op jit(solution)/shard_map/all_to_all | solution.py:79
  45.9 148.4 %copy-start.13 = (f32[128]{0:T(128)}, f32[128]{0:T(128)S(1)}, u32[]{:S(2)}) copy-start(f32[128]{0:T(128)S(1)} %broadcast_multiply_fusion.3) | copy-start | bytes 1540
  46.6 147.7 %copy-start.10 = (f32[128]{0:T(128)}, f32[128]{0:T(128)S(1)}, u32[]{:S(2)}) copy-start(f32[128]{0:T(128)S(1)} %compare_convert_fusion) | copy-start | bytes 1540
  46.9 147.4 %copy-start.42 = (f32[128]{0:T(128)}, f32[128]{0:T(128)S(1)}, u32[]{:S(2)}) copy-start(f32[128]{0:T(128)S(1)} %add_rsqrt_fusion.3) | copy-start | bytes 1540
  208.8 39.0 %all-to-all-start = ((bf16[64,2,1536]{2,1,0:T(2,128)(2,1)}), bf16[64,2,1536]{2,1,0:T(2,128)(2,1)}, u32[]{:S(2)}, u32[]{:S(2)}) async-start(bf16[64,2,1536]{2,1,0:T(2,128)(2,1)} %reshape.130), calls=%async_computation | async-start | bytes 786432 | tf_op jit(solution)/shard_map/all_to_all | solution.py:97
  280.3 46.8 %copy-start.8 = (f32[24]{0:T(128)S(1)}, f32[24]{0:T(128)}, u32[]{:S(2)}) copy-start(f32[24]{0:T(128)} %copy-done.7) | copy-start | bytes 292
  390.5 33.8 %all-to-all-start.2 = ((bf16[64,2,1536]{2,1,0:T(2,128)(2,1)}), bf16[64,2,1536]{2,1,0:T(2,128)(2,1)S(1)}, u32[]{:S(2)}, u32[]{:S(2)}) async-start(bf16[64,2,1536]{2,1,0:T(2,128)(2,1)} %reshape.132), calls=%async_computation.2 | async-start | bytes 786432 | tf_op jit(solution)/shard_map/all_to_all | solution.py:133
  586.1 49.6 %copy-start.9 = (f32[24]{0:T(128)S(1)}, f32[24]{0:T(128)}, u32[]{:S(2)}) copy-start(f32[24]{0:T(128)} %get-tuple-element.111) | copy-start | bytes 292
  595.8 81.9 %copy-start.4 = (f32[1,24,64,128]{3,2,1,0:T(8,128)S(1)}, f32[1,24,64,128]{3,2,1,0:T(8,128)}, u32[]{:S(2)}) copy-start(f32[1,24,64,128]{3,2,1,0:T(8,128)} %copy.64) | copy-start | bytes 2359300
  595.8 39.2 %all-to-all-start.3 = ((bf16[64,2,1536]{2,1,0:T(2,128)(2,1)}), bf16[64,2,1536]{2,1,0:T(2,128)(2,1)S(1)}, u32[]{:S(2)}, u32[]{:S(2)}) async-start(bf16[64,2,1536]{2,1,0:T(2,128)(2,1)} %reshape.134), calls=%async_computation.3 | async-start | bytes 786432 | tf_op jit(solution)/shard_map/all_to_all | solution.py:97
  635.7 67.1 %copy-start.6 = (bf16[1,24,64,128]{3,2,1,0:T(8,128)(2,1)S(1)}, bf16[1,24,64,128]{3,2,1,0:T(8,128)(2,1)}, u32[]{:S(2)}) copy-start(bf16[1,24,64,128]{3,2,1,0:T(8,128)(2,1)} %copy-done.5) | copy-start | bytes 1179652
  677.6 26.7 %copy-start.15 = (f32[24]{0:T(128)S(1)}, f32[24]{0:T(128)}, u32[]{:S(2)}) copy-start(f32[24]{0:T(128)} %get-tuple-element.53) | copy-start | bytes 292
  677.6 26.7 %copy-start.16 = (f32[24]{0:T(128)S(1)}, f32[24]{0:T(128)}, u32[]{:S(2)}) copy-start(f32[24]{0:T(128)} %get-tuple-element.54) | copy-start | bytes 292
  677.7 26.7 %copy-start.17 = (f32[24]{0:T(128)S(1)}, f32[24]{0:T(128)}, u32[]{:S(2)}) copy-start(f32[24]{0:T(128)} %get-tuple-element.55) | copy-start | bytes 292
  680.7 23.7 %copy-start.21 = (f32[24]{0:T(128)S(1)}, f32[24]{0:T(128)}, u32[]{:S(2)}) copy-start(f32[24]{0:T(128)} %get-tuple-element.59) | copy-start | bytes 292
  680.7 23.7 %copy-start.22 = (f32[24]{0:T(128)S(1)}, f32[24]{0:T(128)}, u32[]{:S(2)}) copy-start(f32[24]{0:T(128)} %get-tuple-element.60) | copy-start | bytes 292
  680.7 23.7 %copy-start.23 = (f32[24]{0:T(128)S(1)}, f32[24]{0:T(128)}, u32[]{:S(2)}) copy-start(f32[24]{0:T(128)} %get-tuple-element.61) | copy-start | bytes 292
  680.7 23.7 %copy-start.24 = (f32[24]{0:T(128)S(1)}, f32[24]{0:T(128)}, u32[]{:S(2)}) copy-start(f32[24]{0:T(128)} %get-tuple-element.62) | copy-start | bytes 292
  680.7 23.7 %copy-start.25 = (f32[24]{0:T(128)S(1)}, f32[24]{0:T(128)}, u32[]{:S(2)}) copy-start(f32[24]{0:T(128)} %get-tuple-element.63) | copy-start | bytes 292
  680.7 23.7 %copy-start.26 = (f32[24]{0:T(128)S(1)}, f32[24]{0:T(128)}, u32[]{:S(2)}) copy-start(f32[24]{0:T(128)} %get-tuple-element.64) | copy-start | bytes 292
  680.7 23.7 %copy-start.27 = (f32[24]{0:T(128)S(1)}, f32[24]{0:T(128)}, u32[]{:S(2)}) copy-start(f32[24]{0:T(128)} %get-tuple-element.65) | copy-start | bytes 292
  680.7 23.7 %copy-start.28 = (f32[24]{0:T(128)S(1)}, f32[24]{0:T(128)}, u32[]{:S(2)}) copy-start(f32[24]{0:T(128)} %get-tuple-element.66) | copy-start | bytes 292
  680.8 23.7 %copy-start.29 = (f32[24]{0:T(128)S(1)}, f32[24]{0:T(128)}, u32[]{:S(2)}) copy-start(f32[24]{0:T(128)} %get-tuple-element.67) | copy-start | bytes 292
  680.8 23.7 %copy-start.30 = (f32[24]{0:T(128)S(1)}, f32[24]{0:T(128)}, u32[]{:S(2)}) copy-start(f32[24]{0:T(128)} %get-tuple-element.68) | copy-start | bytes 292
  680.8 23.7 %copy-start.31 = (f32[24]{0:T(128)S(1)}, f32[24]{0:T(128)}, u32[]{:S(2)}) copy-start(f32[24]{0:T(128)} %get-tuple-element.69) | copy-start | bytes 292
  680.8 23.7 %copy-start.32 = (f32[24]{0:T(128)S(1)}, f32[24]{0:T(128)}, u32[]{:S(2)}) copy-start(f32[24]{0:T(128)} %get-tuple-element.70) | copy-start | bytes 292
  680.9 57.0 %copy-start.46 = (f32[24]{0:T(128)S(1)}, f32[24]{0:T(128)}, u32[]{:S(2)}) copy-start(f32[24]{0:T(128)} %get-tuple-element.91) | copy-start | bytes 292
  680.9 56.9 %copy-start.47 = (f32[24]{0:T(128)S(1)}, f32[24]{0:T(128)}, u32[]{:S(2)}) copy-start(f32[24]{0:T(128)} %get-tuple-element.92) | copy-start | bytes 292
  (22 other events, 349.1 us)
Sparse Core Ops, SparseCore 0:
  11.3 176.0 all-gather.3
